TPU v7x, 128 devices: a whole 4x4x4 slice. The times are simulated.
128 devices in a mesh: gz: 16 (over z, y), gy: 8 (over x, core).
Axes of the slice: x: 4, y: 4, z: 4, core: 2. Of those that a mesh axis runs over, the one named last changes fastest.
Arguments:
- species_field: float32 [4, 512, 512, 512], P(None, 'gz', 'gy'), may hold values from -100 to 100
Outputs:
- core_tensor: float32 [4, 512, 4096], P(None, ('gz', 'gy'))
- basis_z: float32 [512, 64], replicated
- basis_y: float32 [512, 64], replicated
All inputs are finite; a program needn't handle non-finite values.
Results may differ from a plain program's by a relative error of at most 0.0003.
Values sent between devices are 32-bit elements; how exact they have to be, the bound alone decides.
A program may use at most 192 MiB of HBM per device.

v0:
```python
import math
import jax
import jax.numpy as jnp
from jax import lax
from jax.sharding import PartitionSpec as P

GRID = 512
RANK = 64
ITERS = 4


def start_table(order, width):
    row_index = jnp.arange(order).astype(jnp.float32)
    col_index = jnp.arange(width).astype(jnp.float32)
    return jnp.cos(math.pi * (row_index[:, None] + 0.5) * col_index[None, :] / order)


def solve_factor(product, inner_gram):
    factor = jnp.linalg.cholesky(inner_gram)
    return lax.linalg.triangular_solve(
        factor, product, left_side=False, lower=True, transpose_a=True
    )


def inner_products(left, right):
    return lax.dot_general(left, right, (((0,), (0,)), ((), ())), precision=lax.Precision.HIGHEST)


def mode_products(left, right, mode):
    others = tuple((d for d in range(4) if d != mode))
    return lax.dot_general(
        left, right, ((others, others), ((), ())), precision=lax.Precision.HIGHEST
    )


def leaf_basis(fibres, mode):
    basis_now = start_table(GRID, RANK)
    gram_total = lax.psum(mode_products(fibres, fibres, mode), ("gz", "gy"))
    for iteration in range(ITERS):
        product = jnp.dot(gram_total, basis_now, precision=lax.Precision.HIGHEST)
        basis_now = solve_factor(product, inner_products(product, product))
    return basis_now


def body(species_field):
    fibres_z = lax.all_to_all(species_field, "gz", split_axis=2, concat_axis=1, tiled=True)
    basis_z = leaf_basis(fibres_z, 1)
    reduced = jnp.einsum("szyx,zr->sryx", fibres_z, basis_z, precision=lax.Precision.HIGHEST)
    mixed = lax.all_to_all(reduced, ("gz", "gy"), split_axis=3, concat_axis=2, tiled=True)
    count_gz = lax.axis_size("gz")
    count_gy = lax.axis_size("gy")
    shape_now = mixed.shape
    y_local = shape_now[2] // (count_gz * count_gy)
    blocks = mixed.reshape(shape_now[0], shape_now[1], count_gz, count_gy, y_local, shape_now[3])
    fibres_y = jnp.transpose(blocks, (0, 1, 3, 2, 4, 5)).reshape(shape_now)
    basis_y = leaf_basis(fibres_y, 2)
    core_tensor = jnp.einsum("sryx,yq->sxrq", fibres_y, basis_y, precision=lax.Precision.HIGHEST)
    core_tensor = core_tensor.reshape(fibres_y.shape[0], fibres_y.shape[3], RANK * RANK)
    return (core_tensor, basis_z, basis_y)


def solution(mesh):
    in_specs = (P(None, "gz", "gy", None),)
    out_specs = (P(None, ("gz", "gy"), None), P(), P())
    return jax.shard_map(body, mesh=mesh, in_specs=in_specs, out_specs=out_specs, check_vma=False)
```

profile of v0, /device:TPU:1, one launch (start us, length us, event | category | flops | bytes accessed | tf_op | source)
XLA Modules:
  0.0 767.0 jit_solution(3029973958028382066)
XLA Ops:
  7.2 15.2 %copy.29 = f32[4,32,64,512]{3,1,0,2:T(8,128)S(1)} copy(f32[4,32,64,512]{3,2,1,0:T(8,128)} %param.4) | data formatting | bytes 33554432 | tf_op args[0]
  22.5 193.2 %all_to_all.33 = f32[4,32,64,512]{3,1,0,2:T(8,128)} all-to-all(f32[4,32,64,512]{3,1,0,2:T(8,128)S(1)} %copy.29), channel_id=1, replica_groups=mesh['gz'=16,'gy'=8] {'gz'}, dimensions={2} | all-to-all | bytes 33554432 | tf_op jit(solution)/shard_map/all_to_all | solution.py:46
  215.6 6.9 copy.30
  222.5 5.7 copy-done
  228.2 28.8 %convolution_bitcast_fusion.2 = f32[512,512]{1,0:T(8,128)} fusion(f32[4,512,4,512]{3,1,2,0:T(8,128)S(1)} %bitcast.170), kind=kOutput, calls=%fused_computation.2 | convolution fusion | flops 25769803776 | bytes 17825792 | tf_op jit(solution)/shard_map/dot_general | solution.py:31
  257.3 146.0 %all-reduce.3.cloned.1.call-done = f32[512,512]{1,0:T(8,128)} async-done(((f32[512,512]{1,0:T(8,128)}), f32[512,512]{1,0:T(8,128)}) %all-reduce.3.cloned.1.call-update) | async-done | bytes 1048592 | tf_op jit(solution)/shard_map/psum | solution.py:38
  403.3 3.4 fusion.1
  407.0 5.8 cholesky.134
  412.9 0.6 compare_reduce_fusion.7
  413.6 0.7 fusion.10
  414.2 4.9 custom-call.12
  419.1 0.3 convolution_bitcast_fusion.9
  419.5 2.4 fusion.53
  422.2 5.8 cholesky.145
  428.1 0.6 compare_reduce_fusion.6
  428.7 0.7 fusion.11
  429.4 4.9 custom-call.13
  434.3 0.3 convolution_bitcast_fusion.8
  434.6 1.1 fusion.55
  436.1 5.8 cholesky.156
  442.0 0.6 compare_reduce_fusion.5
  442.7 0.7 fusion.12
  443.3 4.9 custom-call.14
  448.2 0.3 convolution_bitcast_fusion.7
  448.6 1.1 fusion.57
  450.1 5.8 cholesky.167
  455.9 0.6 compare_reduce_fusion.4
  456.6 1.0 fusion.13
  457.6 4.9 custom-call.15
  462.8 14.2 %convolution_bitcast_fusion = f32[4,64,4,512]{3,1,2,0:T(8,128)S(1)} fusion(f32[4,512,4,512]{3,1,2,0:T(8,128)} %bitcast.171, f32[64,512]{1,0:T(8,128)S(1)} %fusion.27), kind=kOutput, calls=%fused_computation | convolution fusion | flops 3221225472 | bytes 19005440 | tf_op jit(solution)/shard_map/szyx,zr->sryx/dot_general | solution.py:48
  477.1 3.4 copy.35
  480.5 5.3 reshape.76
  485.8 37.2 %all_to_all.34 = f32[128,1,4096]{2,1,0:T(1,128)} all-to-all(f32[128,1,4096]{2,1,0:T(1,128)S(1)} %reshape.76), channel_id=1, replica_groups=mesh['gz'=16,'gy'=8] {'gz','gy'}, dimensions={0} | all-to-all | bytes 4194304 | tf_op jit(solution)/shard_map/all_to_all | solution.py:49
  523.1 0.5 broadcast.80
  523.6 7.3 reduce.4
  530.9 4.3 reshape.77
  535.2 3.5 copy.36
  538.8 2.7 copy.37
  541.5 1.9 copy-done.1
  543.4 8.0 %convolution_bitcast_fusion.1 = f32[512,512]{1,0:T(8,128)} fusion(f32[4,64,512,4]{1,2,3,0:T(8,128)S(1)} %bitcast.172), kind=kOutput, calls=%fused_computation.1 | convolution fusion | flops 3221225472 | bytes 3145728 | tf_op jit(solution)/shard_map/dot_general | solution.py:31
  551.4 143.0 %all-reduce.5.cloned.1.call-done = f32[512,512]{1,0:T(8,128)} async-done(((f32[512,512]{1,0:T(8,128)}), f32[512,512]{1,0:T(8,128)}) %all-reduce.5.cloned.1.call-update) | async-done | bytes 1048592 | tf_op jit(solution)/shard_map/psum | solution.py:38
  694.4 3.6 fusion
  698.4 5.8 cholesky.178
  704.2 0.6 compare_reduce_fusion.3
  704.9 0.7 fusion.14
  705.5 4.9 custom-call.16
  710.8 2.4 fusion.60
  713.5 5.8 cholesky.189
  719.4 0.6 compare_reduce_fusion.2
  720.0 0.7 fusion.15
  720.7 4.9 custom-call.17
  725.6 0.3 convolution_bitcast_fusion.5
  725.9 1.1 fusion.62
  727.4 5.8 cholesky.200
  733.3 0.6 compare_reduce_fusion.1
  734.0 0.7 fusion.16
  734.6 4.9 custom-call.18
  739.9 1.1 fusion.64
  741.4 5.8 cholesky.211
  747.2 0.6 compare_reduce_fusion
  747.9 0.7 fusion.17
  748.5 4.9 custom-call.19
  753.8 4.9 convolution_bitcast_fusion.3
  758.9 0.9 reshape.41
  (53 shorter events, 4.9 us)
Async XLA Ops:
  7.2 396.1 %all-reduce.3.cloned.1.call-start = ((), (), s32[]{:S(2)}) async-start(), calls=%async_computation.2 | async-start | bytes 2097152 | tf_op jit(solution)/shard_map/psum | solution.py:38
  222.5 5.7 copy-start
  257.0 437.4 %all-reduce.5.cloned.1.call-start = ((), (), s32[]{:S(2)}) async-start(), calls=%async_computation.3 | async-start | bytes 2097152 | tf_op jit(solution)/shard_map/psum | solution.py:38
  403.3 31.3 %copy-start.2 = (f32[512,512]{1,0:T(8,128)S(1)}, f32[512,512]{1,0:T(8,128)}, u32[]{:S(2)}) copy-start(f32[512,512]{1,0:T(8,128)} %all-reduce.3.cloned.1.call-done) | copy-start | bytes 3145732
  462.8 14.2 %copy-start.4 = (f32[64,512]{1,0:T(8,128)}, f32[64,512]{1,0:T(8,128)S(1)}, u32[]{:S(2)}) copy-start(f32[64,512]{1,0:T(8,128)S(1)} %fusion.27) | copy-start | bytes 393220
  541.5 1.9 copy-start.1
  694.4 31.5 %copy-start.3 = (f32[512,512]{1,0:T(8,128)S(1)}, f32[512,512]{1,0:T(8,128)}, u32[]{:S(2)}) copy-start(f32[512,512]{1,0:T(8,128)} %all-reduce.5.cloned.1.call-done) | copy-start | bytes 3145732
  753.8 6.0 copy-start.5
Sparse Core Ops, SparseCore 0:
  257.1 146.1 all-reduce.2
  551.5 142.8 all-reduce.4
where the time goes:
time: 776 us; the launch traced here: 767 us
  waiting for transfers between devices  289 us (37%)
  blocking collectives  230 us (30%)
  other arithmetic  104 us (13%)
  matrix products  76.8 us (10%)
  local copies, waits for them, and re-layouts  51.3 us (7%)
  between operations  14.9 us (2%)
    psum x2, waiting for transfers between devices, leaf_basis(): gram_total = lax.psum(mode_products(fibres, fibres, mode), ('gz', 'gy'))  289 us
    all_to_all x1, blocking collectives, body(): lax.all_to_all(species_field, 'gz', split_axis=2, concat_axis=1, tiled=True)  193 us
    another operation x24, other arithmetic, solve_factor(): factor = jnp.linalg.cholesky(inner_gram)  52.2 us
    another operation x16, other arithmetic, solve_factor(): lax.linalg.triangular_solve(factor, product, left_side=False, lower=True,...  44.7 us
    all_to_all x1, blocking collectives, body(): lax.all_to_all(reduced, ('gz', 'gy'), split_axis=3, concat_axis=2, tiled=...  37.2 us
    dot_general x2, matrix products, mode_products(): lax.dot_general(left, right, ((others, others), ((), ())), precision=lax....  36.7 us
    unnamed x15, local copies, waits for them, and re-layouts  32.5 us
    dot_general x8, matrix products, leaf_basis(): product = jnp.dot(gram_total, basis_now, precision=lax.Precision.HIGHEST)  16.2 us
  transfers between devices with their start and end apart: 2, of which 2 were waited for; matrix products, arithmetic and copies ran while one was open for 0% of the time, Pallas kernels for 0%

commit v1 on v0

--- a/solution.py
+++ b/solution.py
@@ -35,7 +35,8 @@
 
 def leaf_basis(fibres, mode):
     basis_now = start_table(GRID, RANK)
-    gram_total = lax.psum(mode_products(fibres, fibres, mode), ("gz", "gy"))
+    inputs = mode_products(fibres, fibres, mode)
+    gram_total = jnp.sum(lax.all_gather(inputs, ("gz", "gy")), 0)
     for iteration in range(ITERS):
         product = jnp.dot(gram_total, basis_now, precision=lax.Precision.HIGHEST)
         basis_now = solve_factor(product, inner_products(product, product))

time: 776 us -> 1130 us (1.46)
  waiting for transfers between devices: 289 us -> 562 us
  other arithmetic: 104 us -> 186 us
    all_gather x0 -> x2, waiting for transfers between devices: none -> 562 us  [leaf_basis(): gram_total = jnp.sum(lax.all_gather(inputs, ('gz', 'gy')), 0)]
    psum x2 -> x0, waiting for transfers between devices: 289 us -> none  [leaf_basis(): gram_total = lax.psum(mode_products(fibres, fibres, mode), ('gz', 'gy'))]
    reduce_sum x0 -> x2, other arithmetic: none -> 81.5 us  [leaf_basis(): gram_total = jnp.sum(lax.all_gather(inputs, ('gz', 'gy')), 0)]
    unnamed x15 -> x11, local copies, waits for them, and re-layouts: 32.5 us -> 32.5 us
where the time goes in v1:
time: 1130 us; the launch traced here: 1120 us
  waiting for transfers between devices  562 us (50%)
  blocking collectives  230 us (20%)
  other arithmetic  186 us (16%)
  matrix products  71.5 us (6%)
  local copies, waits for them, and re-layouts  51.3 us (5%)
  between operations  14.9 us (1%)
    all_gather x2, waiting for transfers between devices, leaf_basis(): gram_total = jnp.sum(lax.all_gather(inputs, ('gz', 'gy')), 0)  562 us
    all_to_all x1, blocking collectives, body(): lax.all_to_all(species_field, 'gz', split_axis=2, concat_axis=1, tiled=True)  193 us
    reduce_sum x2, other arithmetic, leaf_basis(): gram_total = jnp.sum(lax.all_gather(inputs, ('gz', 'gy')), 0)  81.5 us
    another operation x24, other arithmetic, solve_factor(): factor = jnp.linalg.cholesky(inner_gram)  52.2 us
    another operation x16, other arithmetic, solve_factor(): lax.linalg.triangular_solve(factor, product, left_side=False, lower=True,...  44.9 us
    all_to_all x1, blocking collectives, body(): lax.all_to_all(reduced, ('gz', 'gy'), split_axis=3, concat_axis=2, tiled=...  37.2 us
    dot_general x2, matrix products, mode_products(): lax.dot_general(left, right, ((others, others), ((), ())), precision=lax....  36.6 us
    unnamed x11, local copies, waits for them, and re-layouts  32.5 us
  transfers between devices with their start and end apart: 2, of which 2 were waited for; matrix products, arithmetic and copies ran while one was open for 0% of the time, Pallas kernels for 0%

profile of v1, /device:TPU:1, one launch (start us, length us, event | category | flops | bytes accessed | tf_op | source)
XLA Modules:
  0.0 1116.3 jit_solution(7040446045665915288)
XLA Ops:
  7.2 15.2 %copy.29 = f32[4,32,64,512]{3,1,0,2:T(8,128)S(1)} copy(f32[4,32,64,512]{3,2,1,0:T(8,128)} %param.4) | data formatting | bytes 33554432 | tf_op args[0]
  22.5 193.2 %all_to_all.33 = f32[4,32,64,512]{3,1,0,2:T(8,128)} all-to-all(f32[4,32,64,512]{3,1,0,2:T(8,128)S(1)} %copy.29), channel_id=1, replica_groups=mesh['gz'=16,'gy'=8] {'gz'}, dimensions={2} | all-to-all | bytes 33554432 | tf_op jit(solution)/shard_map/all_to_all | solution.py:47
  215.6 6.9 copy.30
  222.5 5.7 copy-done
  228.2 28.7 %convolution_bitcast_fusion.2 = f32[512,512]{1,0:T(8,128)} fusion(f32[4,512,4,512]{3,1,2,0:T(8,128)S(1)} %bitcast.172), kind=kOutput, calls=%fused_computation.2 | convolution fusion | flops 25769803776 | bytes 17825792 | tf_op jit(solution)/shard_map/dot_general | solution.py:31
  257.0 282.7 %all-gather.5.cloned.1.call-done = f32[65536,512]{1,0:T(8,128)} async-done(((f32[512,512]{1,0:T(8,128)}), f32[65536,512]{1,0:T(8,128)}) %all-gather.5.cloned.1.call-update) | async-done | bytes 134217744 | tf_op jit(solution)/shard_map/all_gather | solution.py:39
  539.8 40.7 %reduce_sum.18 = f32[512,512]{1,0:T(8,128)S(1)} reduce(f32[128,512,512]{2,1,0:T(8,128)} %bitcast.5, f32[]{:T(128)} %constant.34.clone.1), dimensions={0}, to_apply=%region_0.0 | reduce | flops 33292288 | bytes 135266304 | tf_op jit(solution)/shard_map/reduce_sum | solution.py:39
  580.5 2.1 fusion.1
  582.9 5.8 cholesky.134
  588.8 0.6 compare_reduce_fusion.7
  589.5 0.7 fusion.10
  590.1 4.9 custom-call.12
  595.0 0.3 convolution_bitcast_fusion.9
  595.4 1.1 fusion.53
  596.9 5.8 cholesky.145
  602.8 0.6 compare_reduce_fusion.6
  603.4 0.7 fusion.11
  604.1 4.9 custom-call.13
  609.0 0.3 convolution_bitcast_fusion.8
  609.3 1.1 fusion.55
  610.8 5.8 cholesky.156
  616.7 0.6 compare_reduce_fusion.5
  617.3 0.7 fusion.12
  618.0 4.9 custom-call.14
  623.2 1.1 fusion.57
  624.7 5.8 cholesky.167
  630.6 0.6 compare_reduce_fusion.4
  631.3 0.7 fusion.13
  631.9 5.2 custom-call.15
  637.5 14.2 %convolution_bitcast_fusion = f32[4,64,4,512]{3,1,2,0:T(8,128)S(1)} fusion(f32[4,512,4,512]{3,1,2,0:T(8,128)} %bitcast.173, f32[64,512]{1,0:T(8,128)S(1)} %fusion.27), kind=kOutput, calls=%fused_computation | convolution fusion | flops 3221225472 | bytes 19005440 | tf_op jit(solution)/shard_map/szyx,zr->sryx/dot_general | solution.py:49
  651.7 3.4 copy.35
  655.1 5.3 reshape.78
  660.5 37.2 %all_to_all.34 = f32[128,1,4096]{2,1,0:T(1,128)} all-to-all(f32[128,1,4096]{2,1,0:T(1,128)S(1)} %reshape.78), channel_id=1, replica_groups=mesh['gz'=16,'gy'=8] {'gz','gy'}, dimensions={0} | all-to-all | bytes 4194304 | tf_op jit(solution)/shard_map/all_to_all | solution.py:50
  697.6 0.5 broadcast.80
  698.2 7.3 reduce.4
  705.5 4.3 reshape.79
  709.8 3.5 copy.36
  713.3 2.7 copy.37
  716.1 1.9 copy-done.1
  718.0 7.9 convolution_bitcast_fusion.1
  725.9 279.5 %all-gather.7.cloned.1.call-done = f32[65536,512]{1,0:T(8,128)} async-done(((f32[512,512]{1,0:T(8,128)}), f32[65536,512]{1,0:T(8,128)}) %all-gather.7.cloned.1.call-update) | async-done | bytes 134217744 | tf_op jit(solution)/shard_map/all_gather | solution.py:39
  1005.5 40.8 %reduce_sum.19 = f32[512,512]{1,0:T(8,128)S(1)} reduce(f32[128,512,512]{2,1,0:T(8,128)} %bitcast.33, f32[]{:T(128)} %constant.34.clone.1), dimensions={0}, to_apply=%region_3.6 | reduce | flops 33292288 | bytes 135266304 | tf_op jit(solution)/shard_map/reduce_sum | solution.py:39
  1046.2 2.1 fusion
  1048.7 5.8 cholesky.178
  1054.5 0.6 compare_reduce_fusion.3
  1055.2 0.7 fusion.14
  1055.8 4.9 custom-call.16
  1061.1 1.1 fusion.60
  1062.6 5.8 cholesky.189
  1068.5 0.6 compare_reduce_fusion.2
  1069.1 0.7 fusion.15
  1069.8 4.9 custom-call.17
  1075.0 1.1 fusion.62
  1076.5 5.8 cholesky.200
  1082.4 0.6 compare_reduce_fusion.1
  1083.0 0.7 fusion.16
  1083.7 4.9 custom-call.18
  1088.9 1.1 fusion.64
  1090.4 5.8 cholesky.211
  1096.3 0.6 compare_reduce_fusion
  1097.0 0.7 fusion.17
  1097.6 5.1 custom-call.19
  1103.0 4.9 convolution_bitcast_fusion.3
  1108.1 0.9 reshape.41
  (51 shorter events, 5.3 us)
Async XLA Ops:
  7.2 532.6 %all-gather.5.cloned.1.call-start = ((), (), s32[]{:S(2)}) async-start(), calls=%async_computation.2 | async-start | bytes 135266304 | tf_op jit(solution)/shard_map/all_gather | solution.py:39
  222.5 5.7 copy-start
  257.0 748.5 %all-gather.7.cloned.1.call-start = ((), (), s32[]{:S(2)}) async-start(), calls=%async_computation.3 | async-start | bytes 135266304 | tf_op jit(solution)/shard_map/all_gather | solution.py:39
  637.5 14.2 %copy-start.2 = (f32[64,512]{1,0:T(8,128)}, f32[64,512]{1,0:T(8,128)S(1)}, u32[]{:S(2)}) copy-start(f32[64,512]{1,0:T(8,128)S(1)} %fusion.27) | copy-start | bytes 393220
  716.0 1.9 copy-start.1
  1103.0 6.0 copy-start.3
Sparse Core Ops, SparseCore 0:
  257.1 282.6 all-gather.4
  726.0 279.3 all-gather.6
